TPU v7x, 32 devices: a whole 2x2x4 slice. The times are simulated.
32 devices in a mesh: tm: 8 (over y, x, core), fsdp: 4 (over z).
Axes of the slice: x: 2, y: 2, z: 4, core: 2. Of those that a mesh axis runs over, the one named last changes fastest.
Arguments:
- frames: bfloat16 [4, 1024, 1024], P('fsdp', 'tm'), may hold values from -6 to 6
- gain_one: float32 [1024], replicated, may hold values from 0.1 to 1.9
- qkv_one: bfloat16 [1024, 3072], P('fsdp'), may hold values from -0.1875 to 0.1875
- out_one: bfloat16 [1024, 1024], P('fsdp'), may hold values from -0.1875 to 0.1875
- gain_two: float32 [1024], replicated, may hold values from 0.1 to 1.9
- qkv_two: bfloat16 [1024, 3072], P('fsdp'), may hold values from -0.1875 to 0.1875
- lengths: int32 [4], P('fsdp'), may hold values from 512 to 1024, as said below
- left_counts: int32 [4], P('fsdp'), may hold values from 0 to 2, as said below
- cotangent: bfloat16 [4, 1024, 1024], P('fsdp', 'tm'), may hold values from -6 to 6
Outputs:
- context: bfloat16 [4, 1024, 1024], P('fsdp', 'tm')
- weight_grad: float32 [1024, 1024], P(('tm', 'fsdp'))
Inputs may be any that keep to these rules, and one draw needn't show every extreme that they name: `lengths`: some utterance is complete in every draw. `left_counts`: in every draw some utterance takes 2 blocks and another none.
All inputs are finite; a program needn't handle non-finite values.
Results may differ from a plain program's by a relative error of at most 0.029.
Values may be sent and summed in bfloat16 or wider, within the bound.
A program may use at most 64 MiB of HBM per device.

v0:
```python
import jax
import jax.numpy as jnp
from jax import lax
from jax.sharding import PartitionSpec as P

HEADS = 16
LEFT_MAX = 2
RIGHT = 23


def from_behind(block, axis, distance):
    devices = range(lax.axis_size(axis))
    route = [(i - distance, i) for i in devices if i - distance in devices]
    return lax.ppermute(block, axis, route)


def norm_rows(values, gain):
    wide = values.astype(jnp.float32)
    mean = jnp.mean(wide, axis=-1, keepdims=True)
    var = jnp.mean((wide - mean) ** 2, axis=-1, keepdims=True)
    return ((wide - mean) * lax.rsqrt(var + 1e-05) * gain).astype(jnp.bfloat16)


def attend(query, keys, values, allowed, heads):
    rows_q, width = query.shape
    head = width // heads
    scale = 1.0 / head**0.5
    q_heads = query.reshape(rows_q, heads, head)
    k_heads = keys.reshape(keys.shape[0], heads, head)
    v_heads = values.reshape(values.shape[0], heads, head)
    scores = (
        jnp.einsum("qhe,khe->hqk", q_heads, k_heads, preferred_element_type=jnp.float32) * scale
    )
    scores = jnp.where(allowed[None], scores, -1e30)
    top = jnp.max(scores, axis=-1, keepdims=True)
    expo = jnp.exp(scores - top)
    weights = (expo / jnp.sum(expo, axis=-1, keepdims=True)).astype(jnp.bfloat16)
    ctx = jnp.einsum("hqk,khe->qhe", weights, v_heads, preferred_element_type=jnp.float32)
    return ctx.reshape(rows_q, width).astype(jnp.bfloat16)


def add_rows(left, piece):
    return jnp.dot(left, piece, preferred_element_type=jnp.float32)


def on_device(
    frames, gain_one, qkv_one, out_one, gain_two, qkv_two, lengths, left_counts, cotangent
):
    local = frames[0]
    grad_in = cotangent[0]
    fr, width = local.shape
    block = lax.axis_index("tm")
    length = lengths[0]
    count = left_counts[0]
    norm_one = norm_rows(local, gain_one)
    proj = add_rows(norm_one, lax.all_gather(qkv_one, "fsdp", axis=0, tiled=True))
    proj = proj.astype(jnp.bfloat16)
    query = proj[:, :width]
    key_value = proj[:, width:]
    earlier = [from_behind(key_value, "tm", step) for step in range(LEFT_MAX, 0, -1)]
    gathered = jnp.concatenate(earlier + [key_value], axis=0)
    rows = jnp.arange(fr, dtype=jnp.int32)
    cols = jnp.arange((LEFT_MAX + 1) * fr, dtype=jnp.int32)
    tpos = block * fr + rows[:, None]
    spos = (block - LEFT_MAX) * fr + cols[None, :]
    apart = LEFT_MAX - cols[None, :] // fr
    allowed = (spos >= 0) & (spos <= tpos) & (apart <= count) & ((spos < length) | (spos == tpos))
    ctx_one = attend(query, gathered[:, :width], gathered[:, width:], allowed, HEADS)
    out_proj = add_rows(ctx_one, lax.all_gather(out_one, "fsdp", axis=0, tiled=True))
    hidden = (local.astype(jnp.float32) + out_proj).astype(jnp.bfloat16)
    norm_two = norm_rows(hidden, gain_two)
    proj2 = add_rows(norm_two, lax.all_gather(qkv_two, "fsdp", axis=0, tiled=True))
    proj2 = proj2.astype(jnp.bfloat16)
    query2 = proj2[:, :width]
    key_value2 = proj2[:, width:]
    ahead = from_behind(key_value2[:RIGHT], "tm", -1)
    joined = jnp.concatenate([key_value2, ahead], axis=0)
    cols2 = jnp.arange(fr + RIGHT, dtype=jnp.int32)
    spos2 = block * fr + cols2[None, :]
    allowed2 = (cols2[None, :] <= rows[:, None] + RIGHT) & ((spos2 < length) | (spos2 == tpos))
    ctx_two = attend(query2, joined[:, :width], joined[:, width:], allowed2, HEADS)
    valid = block * fr + rows < length
    context = jnp.where(valid[:, None], ctx_two, jnp.zeros_like(ctx_two))
    weight_grad = lax.psum_scatter(
        lax.dot_general(
            grad_in, context, (((0,), (0,)), ((), ())), preferred_element_type=jnp.float32
        ),
        ("tm", "fsdp"),
        scatter_dimension=0,
        tiled=True,
    )
    return (context[None], weight_grad)


def solution(mesh):
    in_specs = (
        P("fsdp", "tm", None),
        P(),
        P("fsdp", None),
        P("fsdp", None),
        P(),
        P("fsdp", None),
        P("fsdp"),
        P("fsdp"),
        P("fsdp", "tm", None),
    )
    out_specs = (P("fsdp", "tm", None), P(("tm", "fsdp"), None))
    return jax.shard_map(
        on_device, mesh=mesh, in_specs=in_specs, out_specs=out_specs, check_vma=False
    )
```

profile of v0, /device:TPU:0, one launch (start us, length us, event | category | flops | bytes accessed | tf_op | source)
XLA Modules:
  0.0 462.0 jit_solution(8302980097060515713)
XLA Ops:
  7.2 0.0 copy-start
  7.2 0.0 copy-start.1
  7.2 0.0 copy-start.2
  7.2 0.0 all-gather.4.cloned.1.call-start
  7.2 0.7 all-gather.4.cloned.1.call-update
  7.9 0.0 all-gather.6.cloned.1.call-start
  8.0 0.7 all-gather.6.cloned.1.call-update
  8.7 0.0 all-gather.8.cloned.1.call-start
  8.7 0.7 all-gather.8.cloned.1.call-update
  9.4 0.0 reduce-scatter.4.cloned.1.call-start
  10.8 0.0 copy-done.1
  10.8 0.1 convert_reduce_fusion
  11.0 0.2 fusion.16
  11.2 116.5 %all-gather.4.cloned.1.call-done = bf16[1024,3072]{1,0:T(8,128)(2,1)} async-done(((bf16[256,3072]{1,0:T(8,128)(2,1)}), bf16[1024,3072]{1,0:T(8,128)(2,1)}) %all-gather.4.cloned.1.call-update) | async-done | bytes 6291472 | tf_op jit(solution)/shard_map/all_gather | solution.py:56
  127.7 0.0 copy-done.2
  127.7 3.9 convolution_convert_fusion.1
  131.6 3.4 collective-permute-start
  135.0 1.7 collective-permute-start.1
  136.7 0.1 fusion.30
  136.8 0.1 or_and_fusion
  136.9 0.2 copy.28
  137.1 10.1 %collective-permute-done = bf16[128,2048]{1,0:T(8,128)(2,1)S(1)} collective-permute-done((bf16[128,2048]{1,0:T(8,128)(2,1)S(1)}, bf16[128,2048]{1,0:T(8,128)(2,1)S(1)}, u32[]{:S(2)}, u32[]{:S(2)}) %collective-permute-start) | collective-permute-done | bytes 524320 | tf_op jit(solution)/shard_map/ppermute | solution.py:14
  147.2 0.0 collective-permute-done.1
  147.2 0.1 pad_maximum_fusion
  147.4 0.1 fusion.43
  147.5 0.4 copy.29
  147.8 0.4 copy.27
  148.2 2.9 fusion.44
  151.1 2.8 fusion.10
  153.9 0.0 copy-start.3
  153.9 19.2 %all-gather.6.cloned.1.call-done = bf16[1024,1024]{1,0:T(8,128)(2,1)} async-done(((bf16[256,1024]{1,0:T(8,128)(2,1)}), bf16[1024,1024]{1,0:T(8,128)(2,1)}) %all-gather.6.cloned.1.call-update) | async-done | bytes 2097168 | tf_op jit(solution)/shard_map/all_gather | solution.py:69
  173.1 2.1 fusion.45
  175.3 0.2 multiply_reduce_fusion
  175.5 113.4 %all-gather.8.cloned.1.call-done = bf16[1024,3072]{1,0:T(8,128)(2,1)} async-done(((bf16[256,3072]{1,0:T(8,128)(2,1)}), bf16[1024,3072]{1,0:T(8,128)(2,1)}) %all-gather.8.cloned.1.call-update) | async-done | bytes 6291472 | tf_op jit(solution)/shard_map/all_gather | solution.py:72
  288.9 0.0 copy-done.3
  288.9 3.8 convolution_convert_fusion
  292.7 1.3 collective-permute-start.2
  294.1 0.2 copy.30
  294.3 1.6 collective-permute-done.2
  296.0 0.2 copy.36
  296.2 0.2 copy.35
  296.4 0.7 fusion.46
  297.0 0.4 broadcast_select_fusion.1
  297.4 0.0 copy-done
  297.4 2.6 convolution_bitcast_fusion
  300.0 5.4 %copy.37 = f32[1024,1024]{1,0:T(8,128)} copy(f32[1024,1024]{0,1:T(8,128)} %convolution_bitcast_fusion) | data formatting | bytes 8388608
  305.4 0.0 reduce-scatter.4.cloned.1.call-update
  305.4 0.1 copy.33
  305.6 0.8 broadcast_select_fusion
  306.4 149.1 %reduce-scatter.4.cloned.1.call-done = f32[32,1024]{1,0:T(8,128)} async-done(((f32[1024,1024]{1,0:T(8,128)}), f32[32,1024]{1,0:T(8,128)}) %reduce-scatter.4.cloned.1.call-update) | async-done | bytes 131088
  (17 shorter events, 0.2 us)
Async XLA Ops:
  7.2 290.2 %copy-start = (bf16[1,128,1024]{2,1,0:T(8,128)(2,1)S(1)}, bf16[1,128,1024]{2,1,0:T(8,128)(2,1)}, u32[]{:S(2)}) copy-start(bf16[1,128,1024]{2,1,0:T(8,128)(2,1)} %param.17) | copy-start | bytes 786436
  7.2 3.7 copy-start.1
  7.2 120.5 %copy-start.2 = (f32[1024]{0:T(1024)S(1)}, f32[1024]{0:T(1024)}, u32[]{:S(2)}) copy-start(f32[1024]{0:T(1024)} %param.10) | copy-start | bytes 12292
  7.2 120.5 %all-gather.4.cloned.1.call-start = ((), (), s32[]{:S(2)}) async-start(), calls=%async_computation.1 | async-start | bytes 7864320 | tf_op jit(solution)/shard_map/all_gather | solution.py:56
  7.9 165.2 %all-gather.6.cloned.1.call-start = ((), (), s32[]{:S(2)}) async-start(), calls=%async_computation.2 | async-start | bytes 2621440 | tf_op jit(solution)/shard_map/all_gather | solution.py:69
  8.7 280.2 %all-gather.8.cloned.1.call-start = ((), (), s32[]{:S(2)}) async-start(), calls=%async_computation.3 | async-start | bytes 7864320 | tf_op jit(solution)/shard_map/all_gather | solution.py:72
  9.4 446.0 %reduce-scatter.4.cloned.1.call-start = ((), (), s32[]{:S(2)}) async-start(), calls=%async_computation.4 | async-start | bytes 4325376
  131.6 15.7 %collective-permute-start = (bf16[128,2048]{1,0:T(8,128)(2,1)S(1)}, bf16[128,2048]{1,0:T(8,128)(2,1)S(1)}, u32[]{:S(2)}, u32[]{:S(2)}) collective-permute-start(bf16[128,2048]{1,0:T(8,128)(2,1)S(1)} %slice.37), channel_id=1, source_target_pairs={{0,8},{4,12},{8,16},{12,20},{16,24},{20,28},{1,9},{5,13},{9,17},{1... | collective-permute-start | bytes 1572872 | tf_op jit(solution)/shard_map/ppermute | solution.py:14
  135.0 12.3 %collective-permute-start.1 = (bf16[128,2048]{1,0:T(8,128)(2,1)S(1)}, bf16[128,2048]{1,0:T(8,128)(2,1)S(1)}, u32[]{:S(2)}, u32[]{:S(2)}) collective-permute-start(bf16[128,2048]{1,0:T(8,128)(2,1)S(1)} %slice.37), channel_id=1, source_target_pairs={{0,4},{4,8},{8,12},{12,16},{16,20},{20,24},{24,28},{1,5},{5,9},{9,... | collective-permute-start | bytes 1572872 | tf_op jit(solution)/shard_map/ppermute | solution.py:14
  153.9 135.0 %copy-start.3 = (f32[1024]{0:T(1024)S(1)}, f32[1024]{0:T(1024)}, u32[]{:S(2)}) copy-start(f32[1024]{0:T(1024)} %param.13) | copy-start | bytes 12292
  292.7 3.2 collective-permute-start.2
Sparse Core Ops, SparseCore 0:
  9.6 118.0 all-gather.3
  129.2 43.8 all-gather.5
  174.7 114.1 all-gather.7
  305.5 149.8 reduce-scatter.3
where the time goes:
time: 462 us
  waiting for transfers between devices  412 us (89%)
  matrix products  19.2 us (4%)
  between operations  15.3 us (3%)
  local copies, waits for them, and re-layouts  7.23 us (2%)
  starting transfers between devices  6.51 us (1%)
    unnamed x5, waiting for transfers between devices  151 us
    all_gather x1, waiting for transfers between devices, on_device(): lax.all_gather(qkv_one, 'fsdp', axis=0, tiled=True)  116 us
    all_gather x1, waiting for transfers between devices, on_device(): lax.all_gather(qkv_two, 'fsdp', axis=0, tiled=True)  113 us
    all_gather x1, waiting for transfers between devices, on_device(): lax.all_gather(out_one, 'fsdp', axis=0, tiled=True)  19.2 us
    ppermute x3, waiting for transfers between devices, from_behind(): return lax.ppermute(block, axis, route)  11.7 us
    dot_general x3, matrix products, add_rows(): return jnp.dot(left, piece, preferred_element_type=jnp.float32)  9.84 us
  transfers between devices with their start and end apart: 7, of which 6 were waited for; matrix products, arithmetic and copies ran while one was open for 3% of the time, Pallas kernels for 0%

commit v1 on v0

--- a/solution.py
+++ b/solution.py
@@ -1,6 +1,10 @@
+import functools
+
 import jax
 import jax.numpy as jnp
 from jax import lax
+from jax.experimental import pallas as pl
+from jax.experimental.pallas import tpu as pltpu
 from jax.sharding import PartitionSpec as P
 
 HEADS = 16
@@ -92,7 +96,472 @@
     return (context[None], weight_grad)
 
 
+MESH = pl.DeviceIdType.MESH
+
+
+def flip(index, mask):
+    out, bit = index, 1
+    while bit <= mask:
+        if mask & bit:
+            out = out + bit * (1 - 2 * ((index // bit) % 2))
+        bit *= 2
+    return out
+
+
+def heads_kernel(
+    n,
+    nz,
+    frames_ref, gain_one_ref, qkv_one_ref, out_one_ref, gain_two_ref, qkv_two_ref,
+    length_ref, count_ref, cot_ref,
+    context_ref, grad_ref,
+    nbuf, nbuf2, w1, w2, wo, cotv, cott, q1, k1, v1, ctx1s, ctx1, q2, k2, v2, ctx2s, ctx2,
+    gsend, grecv, gsum, wgr,
+    local_sem, ag_send, ag_recv, ch_send, ch_recv, a2_send, a2_recv, z_send, z_recv,
+):
+    t = lax.axis_index("tm")
+    z = lax.axis_index("fsdp")
+    fr, width = frames_ref.shape
+    cols = width // n
+    head = width // HEADS
+    per = HEADS // n
+    rows = width // nz
+    part = rows // n
+    scale = 1.0 / head**0.5
+    mine = pl.multiple_of(t * cols, cols)
+    chips = n // 2
+
+    def at_cols(index):
+        return pl.ds(pl.multiple_of(index * cols, cols), cols)
+
+    def at_rows(index, size):
+        return pl.ds(pl.multiple_of(index * size, size), size)
+
+    own_rows = at_rows(z, rows)
+    local = []
+    for j in range(3):
+        for which, (src, dst) in enumerate(((qkv_one_ref, w1), (qkv_two_ref, w2))):
+            local.append(
+                pltpu.make_async_copy(
+                    src.at[:, pl.ds(pl.multiple_of(j * width + mine, cols), cols)],
+                    dst.at[own_rows, pl.ds(j * cols, cols)],
+                    local_sem.at[2 * j + which],
+                )
+            )
+    local.append(
+        pltpu.make_async_copy(
+            out_one_ref.at[:, pl.ds(mine, cols)], wo.at[own_rows, pl.ds(mine, cols)], local_sem.at[6]
+        )
+    )
+    local.append(pltpu.make_async_copy(cot_ref, cotv, local_sem.at[7]))
+    for copy in (local[0], local[2], local[4], local[6], local[7], local[1], local[3], local[5]):
+        copy.start()
+
+    barrier = pltpu.get_barrier_semaphore()
+    for d in range(1, n):
+        pl.semaphore_signal(
+            barrier, inc=1, device_id=(lax.rem(t + d, n), z), device_id_type=MESH
+        )
+    for d in range(1, nz):
+        pl.semaphore_signal(
+            barrier, inc=1, device_id=(t, lax.rem(z + d, nz)), device_id_type=MESH
+        )
+    pl.semaphore_wait(barrier, n + nz - 2)
+
+    half = rows // 2
+
+    def chain_view(which, shard, h):
+        span = pl.ds(pl.multiple_of(shard * rows + h * half, half), half)
+        if which == 1:
+            return wo.at[span, pl.ds(mine, cols)]
+        return (w1, None, w2)[which].at[span, :]
+
+    def chain_copy(which, step, up, h):
+        shard = z - step if up else z + step
+        shard = jnp.clip(shard, 0, nz - 1)
+        to = jnp.clip(z + 1 if up else z - 1, 0, nz - 1)
+        view = chain_view(which, shard, h)
+        return pltpu.make_async_remote_copy(
+            src_ref=view,
+            dst_ref=view,
+            send_sem=ch_send.at[which, 0 if up else 1, step, h],
+            recv_sem=ch_recv.at[which, shard, h],
+            device_id=(t, to),
+            device_id_type=MESH,
+        )
+
+    def chain_cond(step, up):
+        if up:
+            return (z >= step) & (z < nz - 1)
+        return (z + step < nz) & (z > 0)
+
+    def chain(which, step):
+        for h in range(2):
+            for up in (True, False):
+                @pl.when(chain_cond(step, up))
+                def _():
+                    copy = chain_copy(which, step, up, h)
+                    if step:
+                        copy.wait_recv()
+                    copy.start()
+
+    def chain_end(which):
+        for edge, up in ((nz - 1, True), (0, False)):
+            @pl.when(z == edge)
+            def _():
+                for step in range(1, nz):
+                    for h in range(2):
+                        shard = edge - step if up else edge + step
+                        view = chain_view(which, shard, h)
+                        pltpu.make_async_remote_copy(
+                            src_ref=view,
+                            dst_ref=view,
+                            send_sem=ch_send.at[which, 0, 0, h],
+                            recv_sem=ch_recv.at[which, shard, h],
+                            device_id=(t, edge - 1 if up else edge + 1),
+                            device_id_type=MESH,
+                        ).wait_recv()
+
+    def chain_sent(which):
+        for step in range(nz - 1):
+            for up in (True, False):
+                for h in range(2):
+                    @pl.when(chain_cond(step, up))
+                    def _():
+                        chain_copy(which, step, up, h).wait_send()
+
+    def ag_view(which, index):
+        if which == 0:
+            return nbuf.at[index]
+        if which == 1:
+            return cott.at[:, at_cols(index)]
+        if which == 2:
+            return wo.at[:, at_cols(index)]
+        return nbuf2.at[index]
+
+    def ag_copy(which, slot):
+        if slot == 0:
+            block, to = t, flip(t, 1)
+        elif slot < chips:
+            block, to = t, flip(t, 2 * slot)
+        else:
+            block, to = flip(t, 2 * (slot - chips + 1)), flip(t, 1)
+        view = ag_view(which, block)
+        return pltpu.make_async_remote_copy(
+            src_ref=view, dst_ref=view,
+            send_sem=ag_send.at[which, slot], recv_sem=ag_recv.at[which, slot],
+            device_id=(to, z), device_id_type=MESH,
+        )
+
+    def ag_wait(which, slot):
+        if slot == 0:
+            block = flip(t, 1)
+        elif slot < chips:
+            block = flip(t, 2 * slot)
+        else:
+            block = flip(t, 2 * (slot - chips + 1) + 1)
+        view = ag_view(which, block)
+        pltpu.make_async_remote_copy(
+            src_ref=view, dst_ref=view,
+            send_sem=ag_send.at[which, slot], recv_sem=ag_recv.at[which, slot],
+            device_id=(flip(t, 1), z), device_id_type=MESH,
+        ).wait_recv()
+
+    def ag_start(which):
+        for slot in list(range(1, chips)) + [0]:
+            ag_copy(which, slot).start()
+
+    def ag_forward(which):
+        for j in range(1, chips):
+            ag_wait(which, j)
+            ag_copy(which, chips + j - 1).start()
+
+    def ag_sent(which):
+        for slot in range(2 * chips - 1):
+            ag_copy(which, slot).wait_send()
+
+    for j in (0, 2, 4):
+        local[j].wait()
+    chain(0, 0)
+    nbuf[t] = norm_rows(frames_ref[...], gain_one_ref[...])
+    ag_start(0)
+    local[6].wait()
+    local[7].wait()
+    turned = cotv[...].T
+    for zz in range(nz):
+        for tt in range(n):
+            cott[zz * rows + tt * part : zz * rows + (tt + 1) * part, pl.ds(mine, cols)] = turned[
+                (tt * nz + zz) * part : (tt * nz + zz + 1) * part
+            ]
+    lead = LEFT_MAX * fr
+    zeros = jnp.zeros((lead, cols), jnp.bfloat16)
+    k1[0:lead, :] = zeros
+    v1[0:lead, :] = zeros
+    k2[n * fr :, :] = zeros[:fr]
+    v2[n * fr :, :] = zeros[:fr]
+    for step in range(1, nz - 1):
+        chain(0, step)
+        chain(1, step - 1)
+    ag_forward(0)
+    ag_start(1)
+    chain(1, nz - 2)
+    for j in (1, 3, 5):
+        local[j].wait()
+    chain(2, 0)
+
+    def project(buf, weight, q, k, v, before, pair):
+        left = buf[pl.ds(pair * 2, 2)].reshape(2 * fr, width)
+        out = jnp.dot(left, weight[...], preferred_element_type=jnp.float32).astype(jnp.bfloat16)
+        span = at_rows(pair, 2 * fr)
+        q[span, :] = out[:, :cols]
+        after = pl.ds(pl.multiple_of(pair * 2 * fr + before, fr), 2 * fr)
+        k[after, :] = out[:, cols : 2 * cols]
+        v[after, :] = out[:, 2 * cols :]
+
+    chain_end(0)
+    ag_wait(0, 0)
+    project(nbuf, w1, q1, k1, v1, lead, t // 2)
+    for j in range(1, chips):
+        ag_wait(0, chips + j - 1)
+        project(nbuf, w1, q1, k1, v1, lead, flip(t, 2 * j) // 2)
+    chain_end(1)
+
+    length = length_ref[0]
+    count = count_ref[0]
+
+    def attend_block(query, keys, values, allowed):
+        lane = lax.broadcasted_iota(jnp.int32, (fr, cols), 1) // head
+        blank = jnp.zeros_like(query)
+        stacked = jnp.concatenate([jnp.where(lane == h, query, blank) for h in range(per)], axis=0)
+        scores = lax.dot_general(
+            stacked, keys, (((1,), (1,)), ((), ())), preferred_element_type=jnp.float32
+        ) * scale
+        scores = scores.reshape(per, fr, keys.shape[0])
+        scores = jnp.where(allowed[None], scores, -1e30)
+        top = jnp.max(scores, axis=-1, keepdims=True)
+        expo = jnp.exp(scores - top)
+        weights = expo * (1.0 / jnp.sum(expo, axis=-1, keepdims=True))
+        weights = weights.astype(jnp.bfloat16).reshape(per * fr, keys.shape[0])
+        mixed = jnp.dot(weights, values, preferred_element_type=jnp.float32)
+        out = mixed[:fr]
+        for h in range(1, per):
+            out = jnp.where(lane == h, mixed[h * fr : (h + 1) * fr], out)
+        return out.astype(jnp.bfloat16)
+
+    def causal(b):
+        span = pl.ds(pl.multiple_of(b * fr, fr), lead + fr)
+        shape = (fr, lead + fr)
+        row = lax.broadcasted_iota(jnp.int32, shape, 0)
+        col = lax.broadcasted_iota(jnp.int32, shape, 1)
+        spos = (b - LEFT_MAX) * fr + col
+        tpos = b * fr + row
+        apart = LEFT_MAX - col // fr
+        allowed = (spos >= 0) & (spos <= tpos) & (apart <= count)
+        allowed = allowed & ((spos < length) | (spos == tpos))
+        return attend_block(q1[at_rows(b, fr), :], k1[span, :], v1[span, :], allowed)
+
+    def ahead(b):
+        span = pl.ds(pl.multiple_of(b * fr, fr), 2 * fr)
+        shape = (fr, 2 * fr)
+        row = lax.broadcasted_iota(jnp.int32, shape, 0)
+        col = lax.broadcasted_iota(jnp.int32, shape, 1)
+        spos = b * fr + col
+        allowed = (col <= row + RIGHT) & ((spos < length) | (col == row))
+        out = attend_block(q2[at_rows(b, fr), :], k2[span, :], v2[span, :], allowed)
+        valid = b * fr + lax.broadcasted_iota(jnp.int32, (fr, cols), 0) < length
+        return jnp.where(valid, out, jnp.zeros_like(out))
+
+    def back_copy(which, d):
+        src, dst = ((ctx1s, ctx1), (ctx2s, ctx2))[which]
+        b = lax.rem(t + d, n)
+        return pltpu.make_async_remote_copy(
+            src_ref=src.at[at_rows(b, fr), :],
+            dst_ref=dst.at[:, pl.ds(mine, cols)],
+            send_sem=a2_send.at[which, d], recv_sem=a2_recv.at[which, d],
+            device_id=(b, z), device_id_type=MESH,
+        )
+
+    def back_wait(which):
+        src, dst = ((ctx1s, ctx1), (ctx2s, ctx2))[which]
+        for d in range(1, n):
+            b = lax.rem(t + n - d, n)
+            pltpu.make_async_remote_copy(
+                src_ref=src.at[at_rows(b, fr), :],
+                dst_ref=dst.at[:, at_cols(b)],
+                send_sem=a2_send.at[which, d], recv_sem=a2_recv.at[which, d],
+                device_id=(b, z), device_id_type=MESH,
+            ).wait_recv()
+
+    def blocks(which, first, last):
+        fun, src = ((causal, ctx1s), (ahead, ctx2s))[which]
+
+        def body(d, carry):
+            b = lax.rem(t + d, n)
+            src[at_rows(b, fr), :] = fun(b)
+            back_copy(which, d).start()
+            return carry
+
+        lax.fori_loop(first, last, body, 0)
+
+    def own_block(which):
+        fun, src, dst = ((causal, ctx1s, ctx1), (ahead, ctx2s, ctx2))[which]
+        out = fun(t)
+        src[at_rows(t, fr), :] = out
+        dst[:, pl.ds(mine, cols)] = out
+
+    ag_start(2)
+    blocks(0, 1, n // 2)
+    ag_forward(1)
+    for step in range(1, nz - 1):
+        chain(2, step)
+    blocks(0, n // 2, n)
+    own_block(0)
+    ag_forward(2)
+    back_wait(0)
+    ag_wait(2, 0)
+    for j in range(1, chips):
+        ag_wait(2, chips + j - 1)
+
+    mixed = jnp.dot(ctx1[...], wo[...], preferred_element_type=jnp.float32)
+    hidden = (frames_ref[...].astype(jnp.float32) + mixed).astype(jnp.bfloat16)
+    nbuf2[t] = norm_rows(hidden, gain_two_ref[...])
+    ag_start(3)
+    chain_end(2)
+    ag_wait(3, 0)
+    project(nbuf2, w2, q2, k2, v2, 0, t // 2)
+    ag_forward(3)
+    for j in range(1, chips):
+        ag_wait(3, chips + j - 1)
+        project(nbuf2, w2, q2, k2, v2, 0, flip(t, 2 * j) // 2)
+    blocks(1, 1, n)
+    own_block(1)
+
+    ag_wait(1, 0)
+    for j in range(1, chips):
+        ag_wait(1, chips + j - 1)
+
+    def term(zz):
+        return jnp.dot(
+            cott[at_rows(zz, rows), :], ctx2s[...], preferred_element_type=jnp.float32
+        )
+
+    def z_copy(d, back):
+        to = lax.rem(z + d, nz)
+        return pltpu.make_async_remote_copy(
+            src_ref=gsend.at[d], dst_ref=grecv.at[d],
+            send_sem=z_send.at[d], recv_sem=z_recv.at[d],
+            device_id=(t, to), device_id_type=MESH,
+        )
+
+    for d in range(1, nz):
+        gsend[d] = term(lax.rem(z + d, nz)).astype(jnp.bfloat16)
+        z_copy(d, False).start()
+    total = term(z)
+    for d in range(1, nz):
+        z_copy(d, True).wait_recv()
+        total = total + grecv[d].astype(jnp.float32)
+    gsum[...] = total
+
+    def g_copy(d):
+        b = lax.rem(t + d, n)
+        return pltpu.make_async_remote_copy(
+            src_ref=gsum.at[at_rows(b, part), :],
+            dst_ref=wgr.at[:, pl.ds(mine, cols)],
+            send_sem=a2_send.at[2, d], recv_sem=a2_recv.at[2, d],
+            device_id=(b, z), device_id_type=MESH,
+        )
+
+    for d in range(1, n):
+        g_copy(d).start()
+    wgr[:, pl.ds(mine, cols)] = gsum[at_rows(t, part), :]
+    back_wait(1)
+    context_ref[...] = ctx2[...]
+    for d in range(1, n):
+        b = lax.rem(t + n - d, n)
+        pltpu.make_async_remote_copy(
+            src_ref=gsum.at[at_rows(b, part), :],
+            dst_ref=wgr.at[:, at_cols(b)],
+            send_sem=a2_send.at[2, d], recv_sem=a2_recv.at[2, d],
+            device_id=(b, z), device_id_type=MESH,
+        ).wait_recv()
+    grad_ref[...] = wgr[...]
+    for which in range(4):
+        ag_sent(which)
+    for which in range(3):
+        chain_sent(which)
+    for d in range(1, n):
+        back_copy(0, d).wait_send()
+        back_copy(1, d).wait_send()
+        g_copy(d).wait_send()
+    for d in range(1, nz):
+        z_copy(d, False).wait_send()
+
+
+def by_heads(
+    n, nz, frames, gain_one, qkv_one, out_one, gain_two, qkv_two, lengths, left_counts, cotangent
+):
+    _, fr, width = frames.shape
+    cols = width // n
+    rows = width // nz
+    span = n * fr
+    vmem = pl.BlockSpec(memory_space=pltpu.VMEM)
+    smem = pl.BlockSpec(memory_space=pltpu.SMEM)
+    hbm = pl.BlockSpec(memory_space=pl.ANY)
+    bf16, f32 = jnp.bfloat16, jnp.float32
+    dma = pltpu.SemaphoreType.DMA
+    context, grad = pl.pallas_call(
+        functools.partial(heads_kernel, n, nz),
+        out_shape=(
+            jax.ShapeDtypeStruct((fr, width), bf16),
+            jax.ShapeDtypeStruct((rows // n, width), f32),
+        ),
+        in_specs=[vmem, vmem, hbm, hbm, vmem, hbm, smem, smem, hbm],
+        out_specs=(vmem, vmem),
+        scratch_shapes=[
+            pltpu.VMEM((n, fr, width), bf16),
+            pltpu.VMEM((n, fr, width), bf16),
+            pltpu.VMEM((width, 3 * cols), bf16),
+            pltpu.VMEM((width, 3 * cols), bf16),
+            pltpu.VMEM((width, width), bf16),
+            pltpu.VMEM((fr, width), bf16),
+            pltpu.VMEM((width, span), bf16),
+            pltpu.VMEM((span, cols), bf16),
+            pltpu.VMEM((span + LEFT_MAX * fr, cols), bf16),
+            pltpu.VMEM((span + LEFT_MAX * fr, cols), bf16),
+            pltpu.VMEM((span, cols), bf16),
+            pltpu.VMEM((fr, width), bf16),
+            pltpu.VMEM((span, cols), bf16),
+            pltpu.VMEM((span + fr, cols), bf16),
+            pltpu.VMEM((span + fr, cols), bf16),
+            pltpu.VMEM((span, cols), bf16),
+            pltpu.VMEM((fr, width), bf16),
+            pltpu.VMEM((nz, rows, cols), bf16),
+            pltpu.VMEM((nz, rows, cols), bf16),
+            pltpu.VMEM((rows, cols), f32),
+            pltpu.VMEM((rows // n, width), f32),
+            dma((8,)),
+            dma((4, n - 1)),
+            dma((4, n - 1)),
+            dma((3, 2, nz, 2)),
+            dma((3, nz, 2)),
+            dma((3, n)),
+            dma((3, n)),
+            dma((nz,)),
+            dma((nz,)),
+        ],
+        compiler_params=pltpu.CompilerParams(
+            collective_id=0, has_side_effects=True, vmem_limit_bytes=60 * 1024 * 1024
+        ),
+    )(
+        frames[0], gain_one[None], qkv_one, out_one, gain_two[None], qkv_two,
+        lengths, left_counts, cotangent[0],
+    )
+    return (context[None], grad)
+
+
 def solution(mesh):
+    n_tm = mesh.shape["tm"]
+    even = n_tm > 2 and n_tm & (n_tm - 1) == 0 and HEADS % n_tm == 0
+    chosen = functools.partial(by_heads, n_tm, mesh.shape["fsdp"]) if even else on_device
     in_specs = (
         P("fsdp", "tm", None),
         P(),
@@ -106,5 +575,5 @@
     )
     out_specs = (P("fsdp", "tm", None), P(("tm", "fsdp"), None))
     return jax.shard_map(
-        on_device, mesh=mesh, in_specs=in_specs, out_specs=out_specs, check_vma=False
+        chosen, mesh=mesh, in_specs=in_specs, out_specs=out_specs, check_vma=False
     )

time: 462 us -> 85.7 us (0.19)
  waiting for transfers between devices: 412 us -> 0 us
  Pallas kernels: 0 us -> 80.4 us
  matrix products: 19.2 us -> 0 us
  between operations: 15.3 us -> 1.93 us
  starting transfers between devices: 6.51 us -> 0 us
    all_gather x3 -> x0, waiting for transfers between devices: 249 us -> none  [the longest x1 116 us: on_device(): lax.all_gather(qkv_one, 'fsdp', axis=0, tiled=True)]
    unnamed x5 -> x0, waiting for transfers between devices: 151 us -> none
    pallas_call x0 -> x1, Pallas kernels: none -> 80.4 us  [by_heads(): pl.pallas_call(functools.partial(heads_kernel, n, nz), out_shape=(jax.Sha...]
    dot_general x6 -> x0, matrix products: 15.6 us -> none  [the longest x3 9.84 us: add_rows(): return jnp.dot(left, piece, preferred_element_type=jnp.float32)]
    ppermute x3 -> x0, waiting for transfers between devices: 11.7 us -> none  [from_behind(): return lax.ppermute(block, axis, route)]
    ppermute x3 -> x0, starting transfers between devices: 6.36 us -> none  [from_behind(): return lax.ppermute(block, axis, route)]
  transfers between devices with their start and end apart: 7 -> 0, of which waited for: 6 -> 0; matrix products, arithmetic and copies ran while one was open for 3% -> 0% of each run, Pallas kernels for 0% -> 0%
where the time goes in v1:
time: 85.7 us; the launch traced here: 85.5 us
  Pallas kernels  80.4 us (94%)
  local copies, waits for them, and re-layouts  3.24 us (4%)
  between operations  1.93 us (2%)
    pallas_call x1, Pallas kernels, by_heads(): pl.pallas_call(functools.partial(heads_kernel, n, nz), out_shape=(jax.Sha...  80.4 us
    unnamed x2, local copies, waits for them, and re-layouts  3.24 us

profile of v1, /device:TPU:0, one launch (start us, length us, event | category | flops | bytes accessed | tf_op | source)
XLA Modules:
  0.0 85.5 jit_solution(10883739145000141490)
XLA Ops:
  1.9 80.4 %shard_map.104 = (bf16[128,1024]{1,0:T(8,128)(2,1)}, f32[32,1024]{1,0:T(8,128)}) custom-call(bf16[128,1024]{1,0:T(8,128)(2,1)} %bitcast.5, f32[1,1024]{1,0:T(1,128)} %bitcast.8, bf16[256,3072]{1,0:T(8,128)(2,1)} %qkv_one_ref.1, bf16[256,1024]{1,0:T(8,128)(2,1)} %out_one_ref.1, f32[1,1024]{1,0:T(1,128)} %bitcast.9, bf16[256,3072]{1,0:T(8,128)(2,1)} %qkv_two_ref.1, ...), custom_call_target="tpu_custom_call" | custom-call | tf_op jit(solution)/shard_map/pallas_call | solution.py:511
  82.3 1.7 %copy.15 = bf16[1,128,1024]{2,1,0:T(8,128)(2,1)} copy(bf16[1,128,1024]{2,1,0:T(8,128)(2,1)} %bitcast.7) | data formatting | bytes 524288
  84.0 1.6 %copy.16 = f32[32,1024]{1,0:T(8,128)} copy(f32[32,1024]{1,0:T(8,128)} %get-tuple-element.9) | data formatting | bytes 262144

commit v2 on v1

--- a/solution.py
+++ b/solution.py
@@ -10,6 +10,7 @@
 HEADS = 16
 LEFT_MAX = 2
 RIGHT = 23
+CHIPS = 4
 
 
 def from_behind(block, axis, distance):
@@ -128,7 +129,6 @@
     part = rows // n
     scale = 1.0 / head**0.5
     mine = pl.multiple_of(t * cols, cols)
-    chips = n // 2
 
     def at_cols(index):
         return pl.ds(pl.multiple_of(index * cols, cols), cols)
@@ -153,7 +153,7 @@
         )
     )
     local.append(pltpu.make_async_copy(cot_ref, cotv, local_sem.at[7]))
-    for copy in (local[0], local[2], local[4], local[6], local[7], local[1], local[3], local[5]):
+    for copy in (local[6], local[0], local[2], local[4], local[7], local[1], local[3], local[5]):
         copy.start()
 
     barrier = pltpu.get_barrier_semaphore()
@@ -229,62 +229,67 @@
                     def _():
                         chain_copy(which, step, up, h).wait_send()
 
-    def ag_view(which, index):
-        if which == 0:
-            return nbuf.at[index]
-        if which == 1:
-            return cott.at[:, at_cols(index)]
-        if which == 2:
-            return wo.at[:, at_cols(index)]
-        return nbuf2.at[index]
+    def ag_view(which, index, piece):
+        if which in (0, 3):
+            buf = (nbuf, None, None, nbuf2)[which]
+            if piece is None:
+                return buf.at[index]
+            return buf.at[index, pl.ds(piece * (fr // 2), fr // 2), :]
+        buf = (None, cott, wo)[which]
+        if piece is None:
+            return buf.at[:, at_cols(index)]
+        return buf.at[pl.ds(piece * (width // 2), width // 2), at_cols(index)]
+
+    slots = (
+        (0, None, 1), (0, 0, 2), (0, 1, 2), (0, 1, 4), (0, 0, 4),
+        (2, 0, 4), (4, 1, 2),
+        (2, None, 1), (4, None, 1), (6, 0, 1), (6, 1, 1),
+    )
 
     def ag_copy(which, slot):
-        if slot == 0:
-            block, to = t, flip(t, 1)
-        elif slot < chips:
-            block, to = t, flip(t, 2 * slot)
-        else:
-            block, to = flip(t, 2 * (slot - chips + 1)), flip(t, 1)
-        view = ag_view(which, block)
+        block, piece, to = slots[slot]
+        view = ag_view(which, flip(t, block), piece)
         return pltpu.make_async_remote_copy(
             src_ref=view, dst_ref=view,
             send_sem=ag_send.at[which, slot], recv_sem=ag_recv.at[which, slot],
-            device_id=(to, z), device_id_type=MESH,
+            device_id=(flip(t, to), z), device_id_type=MESH,
         )
 
     def ag_wait(which, slot):
-        if slot == 0:
-            block = flip(t, 1)
-        elif slot < chips:
-            block = flip(t, 2 * slot)
-        else:
-            block = flip(t, 2 * (slot - chips + 1) + 1)
-        view = ag_view(which, block)
+        block, piece, to = slots[slot]
+        view = ag_view(which, flip(t, block ^ to), piece)
         pltpu.make_async_remote_copy(
             src_ref=view, dst_ref=view,
             send_sem=ag_send.at[which, slot], recv_sem=ag_recv.at[which, slot],
-            device_id=(flip(t, 1), z), device_id_type=MESH,
+            device_id=(flip(t, to), z), device_id_type=MESH,
         ).wait_recv()
 
     def ag_start(which):
-        for slot in list(range(1, chips)) + [0]:
+        for slot in (1, 3, 2, 4, 0):
             ag_copy(which, slot).start()
 
-    def ag_forward(which):
-        for j in range(1, chips):
-            ag_wait(which, j)
-            ag_copy(which, chips + j - 1).start()
+    def ag_forward(which, stage):
+        for waits, slot in (
+            (((1, 5), (3, 6)), ((2, 7), (4, 8)), ((5, 9), (6, 10)))[stage]
+        ):
+            ag_wait(which, waits)
+            ag_copy(which, slot).start()
+
+    def ag_partner(which):
+        for slot in (0, 7, 8, 9, 10):
+            ag_wait(which, slot)
 
     def ag_sent(which):
-        for slot in range(2 * chips - 1):
+        for slot in range(len(slots)):
             ag_copy(which, slot).wait_send()
 
+    local[6].wait()
+    chain(1, 0)
     for j in (0, 2, 4):
         local[j].wait()
     chain(0, 0)
     nbuf[t] = norm_rows(frames_ref[...], gain_one_ref[...])
     ag_start(0)
-    local[6].wait()
     local[7].wait()
     turned = cotv[...].T
     for zz in range(nz):
@@ -298,12 +303,17 @@
     v1[0:lead, :] = zeros
     k2[n * fr :, :] = zeros[:fr]
     v2[n * fr :, :] = zeros[:fr]
-    for step in range(1, nz - 1):
+    chain(1, 1)
+    ag_forward(0, 0)
+    for step in range(2, nz - 1):
+        chain(1, step)
+    chain_end(1)
+    ag_forward(0, 1)
+    chain(0, 1)
+    ag_forward(0, 2)
+    ag_start(2)
+    for step in range(2, nz - 1):
         chain(0, step)
-        chain(1, step - 1)
-    ag_forward(0)
-    ag_start(1)
-    chain(1, nz - 2)
     for j in (1, 3, 5):
         local[j].wait()
     chain(2, 0)
@@ -317,13 +327,14 @@
         k[after, :] = out[:, cols : 2 * cols]
         v[after, :] = out[:, 2 * cols :]
 
+    ag_forward(2, 0)
+    ag_forward(2, 1)
+    ag_partner(0)
+    ag_forward(2, 2)
+    ag_start(1)
     chain_end(0)
-    ag_wait(0, 0)
-    project(nbuf, w1, q1, k1, v1, lead, t // 2)
-    for j in range(1, chips):
-        ag_wait(0, chips + j - 1)
-        project(nbuf, w1, q1, k1, v1, lead, flip(t, 2 * j) // 2)
-    chain_end(1)
+    for j in range(n // 2):
+        project(nbuf, w1, q1, k1, v1, lead, j)
 
     length = length_ref[0]
     count = count_ref[0]
@@ -408,36 +419,38 @@
         src[at_rows(t, fr), :] = out
         dst[:, pl.ds(mine, cols)] = out
 
-    ag_start(2)
     blocks(0, 1, n // 2)
-    ag_forward(1)
-    for step in range(1, nz - 1):
-        chain(2, step)
+    ag_forward(1, 0)
+    chain(2, 1)
     blocks(0, n // 2, n)
     own_block(0)
-    ag_forward(2)
+    ag_forward(1, 1)
+    ag_partner(2)
     back_wait(0)
-    ag_wait(2, 0)
-    for j in range(1, chips):
-        ag_wait(2, chips + j - 1)
 
     mixed = jnp.dot(ctx1[...], wo[...], preferred_element_type=jnp.float32)
     hidden = (frames_ref[...].astype(jnp.float32) + mixed).astype(jnp.bfloat16)
     nbuf2[t] = norm_rows(hidden, gain_two_ref[...])
     ag_start(3)
+    ag_forward(1, 2)
+    for step in range(2, nz - 1):
+        chain(2, step)
+    ag_forward(3, 0)
     chain_end(2)
     ag_wait(3, 0)
     project(nbuf2, w2, q2, k2, v2, 0, t // 2)
-    ag_forward(3)
-    for j in range(1, chips):
-        ag_wait(3, chips + j - 1)
-        project(nbuf2, w2, q2, k2, v2, 0, flip(t, 2 * j) // 2)
+    ag_forward(3, 1)
+    ag_wait(3, 7)
+    project(nbuf2, w2, q2, k2, v2, 0, flip(t, 2) // 2)
+    ag_wait(3, 8)
+    project(nbuf2, w2, q2, k2, v2, 0, flip(t, 4) // 2)
+    ag_forward(3, 2)
+    ag_wait(3, 9)
+    ag_wait(3, 10)
+    project(nbuf2, w2, q2, k2, v2, 0, flip(t, 6) // 2)
     blocks(1, 1, n)
     own_block(1)
-
-    ag_wait(1, 0)
-    for j in range(1, chips):
-        ag_wait(1, chips + j - 1)
+    ag_partner(1)
 
     def term(zz):
         return jnp.dot(
@@ -494,6 +507,11 @@
         g_copy(d).wait_send()
     for d in range(1, nz):
         z_copy(d, False).wait_send()
+
+
+def hand_out(context_ref, grad_ref, context_out, grad_out):
+    context_out[...] = context_ref[...]
+    grad_out[...] = grad_ref[...]
 
 
 def by_heads(
@@ -539,8 +557,8 @@
             pltpu.VMEM((rows, cols), f32),
             pltpu.VMEM((rows // n, width), f32),
             dma((8,)),
-            dma((4, n - 1)),
-            dma((4, n - 1)),
+            dma((4, 11)),
+            dma((4, 11)),
             dma((3, 2, nz, 2)),
             dma((3, nz, 2)),
             dma((3, n)),
@@ -555,12 +573,21 @@
         frames[0], gain_one[None], qkv_one, out_one, gain_two[None], qkv_two,
         lengths, left_counts, cotangent[0],
     )
+    context, grad = pl.pallas_call(
+        hand_out,
+        out_shape=(
+            jax.ShapeDtypeStruct((fr, width), bf16),
+            jax.ShapeDtypeStruct((rows // n, width), f32),
+        ),
+        in_specs=[vmem, vmem],
+        out_specs=(vmem, vmem),
+    )(context, grad)
     return (context[None], grad)
 
 
 def solution(mesh):
     n_tm = mesh.shape["tm"]
-    even = n_tm > 2 and n_tm & (n_tm - 1) == 0 and HEADS % n_tm == 0
+    even = n_tm == 2 * CHIPS and HEADS % n_tm == 0
     chosen = functools.partial(by_heads, n_tm, mesh.shape["fsdp"]) if even else on_device
     in_specs = (
         P("fsdp", "tm", None),

time: 85.7 us -> 73.4 us (0.86)
  Pallas kernels: 80.4 us -> 71.3 us
  local copies, waits for them, and re-layouts: 3.24 us -> 0 us
    pallas_call x1, Pallas kernels: 80.4 us -> 69.6 us  [by_heads(): pl.pallas_call(functools.partial(heads_kernel, n, nz), out_shape=(jax.Sha...]
    unnamed x2 -> x0, local copies, waits for them, and re-layouts: 3.24 us -> none
    pallas_call x0 -> x1, Pallas kernels: none -> 1.74 us  [by_heads(): pl.pallas_call(hand_out, out_shape=(jax.ShapeDtypeStruct((fr, width), bf1...]
where the time goes in v2:
time: 73.4 us; the launch traced here: 73.2 us
  Pallas kernels  71.3 us (97%)
  between operations  1.93 us (3%)
    pallas_call x1, Pallas kernels, by_heads(): pl.pallas_call(functools.partial(heads_kernel, n, nz), out_shape=(jax.Sha...  69.6 us
    pallas_call x1, Pallas kernels, by_heads(): pl.pallas_call(hand_out, out_shape=(jax.ShapeDtypeStruct((fr, width), bf1...  1.74 us

profile of v2, /device:TPU:0, one launch (start us, length us, event | category | flops | bytes accessed | tf_op | source)
XLA Modules:
  0.0 73.2 jit_solution(10736624974003319211)
XLA Ops:
  1.9 69.6 %shard_map.104 = (bf16[128,1024]{1,0:T(8,128)(2,1)}, f32[32,1024]{1,0:T(8,128)}) custom-call(bf16[128,1024]{1,0:T(8,128)(2,1)} %bitcast.5, f32[1,1024]{1,0:T(1,128)} %bitcast.7, bf16[256,3072]{1,0:T(8,128)(2,1)} %qkv_one_ref.1, bf16[256,1024]{1,0:T(8,128)(2,1)} %out_one_ref.1, f32[1,1024]{1,0:T(1,128)} %bitcast.8, bf16[256,3072]{1,0:T(8,128)(2,1)} %qkv_two_ref.1, ...), custom_call_target="tpu_custom_call" | custom-call | tf_op jit(solution)/shard_map/pallas_call | solution.py:529
  71.5 1.7 %shard_map.105 = (bf16[128,1024]{1,0:T(8,128)(2,1)}, f32[32,1024]{1,0:T(8,128)}) custom-call(bf16[128,1024]{1,0:T(8,128)(2,1)} %get-tuple-element.6.context_ref, f32[32,1024]{1,0:T(8,128)} %get-tuple-element.7.grad_ref), custom_call_target="tpu_custom_call" | custom-call | tf_op jit(solution)/shard_map/pallas_call | solution.py:576

commit v3 on v2

--- a/solution.py
+++ b/solution.py
@@ -149,7 +149,7 @@
             )
     local.append(
         pltpu.make_async_copy(
-            out_one_ref.at[:, pl.ds(mine, cols)], wo.at[own_rows, pl.ds(mine, cols)], local_sem.at[6]
+            out_one_ref, wo.at[pl.ds(0, rows), :], local_sem.at[6]
         )
     )
     local.append(pltpu.make_async_copy(cot_ref, cotv, local_sem.at[7]))
@@ -169,8 +169,9 @@
 
     half = rows // 2
 
-    def chain_view(which, shard, h):
-        span = pl.ds(pl.multiple_of(shard * rows + h * half, half), half)
+    def chain_view(which, shard, h, at):
+        place = lax.rem(shard - at + nz, nz) if which == 1 else shard
+        span = pl.ds(pl.multiple_of(place * rows + h * half, half), half)
         if which == 1:
             return wo.at[span, pl.ds(mine, cols)]
         return (w1, None, w2)[which].at[span, :]
@@ -179,15 +180,25 @@
         shard = z - step if up else z + step
         shard = jnp.clip(shard, 0, nz - 1)
         to = jnp.clip(z + 1 if up else z - 1, 0, nz - 1)
-        view = chain_view(which, shard, h)
         return pltpu.make_async_remote_copy(
-            src_ref=view,
-            dst_ref=view,
+            src_ref=chain_view(which, shard, h, z),
+            dst_ref=chain_view(which, shard, h, to),
             send_sem=ch_send.at[which, 0 if up else 1, step, h],
             recv_sem=ch_recv.at[which, shard, h],
             device_id=(t, to),
             device_id_type=MESH,
         )
+
+    def chain_wait(which, shard, h, other):
+        view = chain_view(which, shard, h, z)
+        pltpu.make_async_remote_copy(
+            src_ref=view,
+            dst_ref=view,
+            send_sem=ch_send.at[which, 0, 0, h],
+            recv_sem=ch_recv.at[which, shard, h],
+            device_id=(t, other),
+            device_id_type=MESH,
+        ).wait_recv()
 
     def chain_cond(step, up):
         if up:
@@ -201,7 +212,7 @@
                 def _():
                     copy = chain_copy(which, step, up, h)
                     if step:
-                        copy.wait_recv()
+                        chain_wait(which, z - step if up else z + step, h, z + 1 if up else z - 1)
                     copy.start()
 
     def chain_end(which):
@@ -211,15 +222,7 @@
                 for step in range(1, nz):
                     for h in range(2):
                         shard = edge - step if up else edge + step
-                        view = chain_view(which, shard, h)
-                        pltpu.make_async_remote_copy(
-                            src_ref=view,
-                            dst_ref=view,
-                            send_sem=ch_send.at[which, 0, 0, h],
-                            recv_sem=ch_recv.at[which, shard, h],
-                            device_id=(t, edge - 1 if up else edge + 1),
-                            device_id_type=MESH,
-                        ).wait_recv()
+                        chain_wait(which, shard, h, edge - 1 if up else edge + 1)
 
     def chain_sent(which):
         for step in range(nz - 1):
@@ -235,10 +238,11 @@
             if piece is None:
                 return buf.at[index]
             return buf.at[index, pl.ds(piece * (fr // 2), fr // 2), :]
-        buf = (None, cott, wo)[which]
+        buf, first = ((None, 0), (cott, 0), (wo, rows))[which]
+        size = width - first
         if piece is None:
-            return buf.at[:, at_cols(index)]
-        return buf.at[pl.ds(piece * (width // 2), width // 2), at_cols(index)]
+            return buf.at[pl.ds(first, size), at_cols(index)]
+        return buf.at[pl.ds(first + piece * (size // 2), size // 2), at_cols(index)]
 
     slots = (
         (0, None, 1), (0, 0, 2), (0, 1, 2), (0, 1, 4), (0, 0, 4),
@@ -283,11 +287,10 @@
         for slot in range(len(slots)):
             ag_copy(which, slot).wait_send()
 
-    local[6].wait()
-    chain(1, 0)
     for j in (0, 2, 4):
         local[j].wait()
     chain(0, 0)
+    local[6].wait()
     nbuf[t] = norm_rows(frames_ref[...], gain_one_ref[...])
     ag_start(0)
     local[7].wait()
@@ -303,17 +306,15 @@
     v1[0:lead, :] = zeros
     k2[n * fr :, :] = zeros[:fr]
     v2[n * fr :, :] = zeros[:fr]
+    ag_forward(0, 0)
+    chain(0, 1)
+    chain(1, 0)
+    ag_forward(0, 1)
+    chain(0, 2)
+    ag_forward(0, 2)
+    ag_start(1)
     chain(1, 1)
-    ag_forward(0, 0)
-    for step in range(2, nz - 1):
-        chain(1, step)
-    chain_end(1)
-    ag_forward(0, 1)
-    chain(0, 1)
-    ag_forward(0, 2)
-    ag_start(2)
-    for step in range(2, nz - 1):
-        chain(0, step)
+    chain(1, 2)
     for j in (1, 3, 5):
         local[j].wait()
     chain(2, 0)
@@ -327,14 +328,14 @@
         k[after, :] = out[:, cols : 2 * cols]
         v[after, :] = out[:, 2 * cols :]
 
-    ag_forward(2, 0)
-    ag_forward(2, 1)
     ag_partner(0)
-    ag_forward(2, 2)
-    ag_start(1)
     chain_end(0)
+    ag_forward(1, 0)
     for j in range(n // 2):
         project(nbuf, w1, q1, k1, v1, lead, j)
+    chain_end(1)
+    ag_start(2)
+    ag_forward(1, 1)
 
     length = length_ref[0]
     count = count_ref[0]
@@ -381,12 +382,15 @@
         valid = b * fr + lax.broadcasted_iota(jnp.int32, (fr, cols), 0) < length
         return jnp.where(valid, out, jnp.zeros_like(out))
 
+    def turned_cols(which, index):
+        return lax.rem(index - z * (rows // cols) + n, n) if which == 0 else index
+
     def back_copy(which, d):
         src, dst = ((ctx1s, ctx1), (ctx2s, ctx2))[which]
         b = lax.rem(t + d, n)
         return pltpu.make_async_remote_copy(
             src_ref=src.at[at_rows(b, fr), :],
-            dst_ref=dst.at[:, pl.ds(mine, cols)],
+            dst_ref=dst.at[:, at_cols(turned_cols(which, t))],
             send_sem=a2_send.at[which, d], recv_sem=a2_recv.at[which, d],
             device_id=(b, z), device_id_type=MESH,
         )
@@ -397,7 +401,7 @@
             b = lax.rem(t + n - d, n)
             pltpu.make_async_remote_copy(
                 src_ref=src.at[at_rows(b, fr), :],
-                dst_ref=dst.at[:, at_cols(b)],
+                dst_ref=dst.at[:, at_cols(turned_cols(which, b))],
                 send_sem=a2_send.at[which, d], recv_sem=a2_recv.at[which, d],
                 device_id=(b, z), device_id_type=MESH,
             ).wait_recv()
@@ -417,14 +421,16 @@
         fun, src, dst = ((causal, ctx1s, ctx1), (ahead, ctx2s, ctx2))[which]
         out = fun(t)
         src[at_rows(t, fr), :] = out
-        dst[:, pl.ds(mine, cols)] = out
+        dst[:, at_cols(turned_cols(which, t))] = out
 
     blocks(0, 1, n // 2)
-    ag_forward(1, 0)
+    ag_forward(1, 2)
     chain(2, 1)
     blocks(0, n // 2, n)
     own_block(0)
-    ag_forward(1, 1)
+    ag_forward(2, 0)
+    ag_forward(2, 1)
+    ag_forward(2, 2)
     ag_partner(2)
     back_wait(0)
 
@@ -432,7 +438,6 @@
     hidden = (frames_ref[...].astype(jnp.float32) + mixed).astype(jnp.bfloat16)
     nbuf2[t] = norm_rows(hidden, gain_two_ref[...])
     ag_start(3)
-    ag_forward(1, 2)
     for step in range(2, nz - 1):
         chain(2, step)
     ag_forward(3, 0)
@@ -587,7 +592,7 @@
 
 def solution(mesh):
     n_tm = mesh.shape["tm"]
-    even = n_tm == 2 * CHIPS and HEADS % n_tm == 0
+    even = n_tm == 2 * CHIPS and mesh.shape["fsdp"] == CHIPS and HEADS % n_tm == 0
     chosen = functools.partial(by_heads, n_tm, mesh.shape["fsdp"]) if even else on_device
     in_specs = (
         P("fsdp", "tm", None),

time: 73.4 us -> 70.6 us (0.962)
  Pallas kernels: 71.3 us -> 68.5 us
    pallas_call x1, Pallas kernels: 69.6 us -> 66.8 us  [by_heads(): pl.pallas_call(functools.partial(heads_kernel, n, nz), out_shape=(jax.Sha...]
where the time goes in v3:
time: 70.6 us; the launch traced here: 70.5 us
  Pallas kernels  68.5 us (97%)
  between operations  1.93 us (3%)
    pallas_call x1, Pallas kernels, by_heads(): pl.pallas_call(functools.partial(heads_kernel, n, nz), out_shape=(jax.Sha...  66.8 us
    pallas_call x1, Pallas kernels, by_heads(): pl.pallas_call(hand_out, out_shape=(jax.ShapeDtypeStruct((fr, width), bf1...  1.74 us

profile of v3, /device:TPU:0, one launch (start us, length us, event | category | flops | bytes accessed | tf_op | source)
XLA Modules:
  0.0 70.5 jit_solution(7808191045961995028)
XLA Ops:
  1.9 66.8 %shard_map.104 = (bf16[128,1024]{1,0:T(8,128)(2,1)}, f32[32,1024]{1,0:T(8,128)}) custom-call(bf16[128,1024]{1,0:T(8,128)(2,1)} %bitcast.5, f32[1,1024]{1,0:T(1,128)} %bitcast.7, bf16[256,3072]{1,0:T(8,128)(2,1)} %qkv_one_ref.1, bf16[256,1024]{1,0:T(8,128)(2,1)} %out_one_ref.1, f32[1,1024]{1,0:T(1,128)} %bitcast.8, bf16[256,3072]{1,0:T(8,128)(2,1)} %qkv_two_ref.1, ...), custom_call_target="tpu_custom_call" | custom-call | tf_op jit(solution)/shard_map/pallas_call | solution.py:534
  68.7 1.7 %shard_map.105 = (bf16[128,1024]{1,0:T(8,128)(2,1)}, f32[32,1024]{1,0:T(8,128)}) custom-call(bf16[128,1024]{1,0:T(8,128)(2,1)} %get-tuple-element.6.context_ref, f32[32,1024]{1,0:T(8,128)} %get-tuple-element.7.grad_ref), custom_call_target="tpu_custom_call" | custom-call | tf_op jit(solution)/shard_map/pallas_call | solution.py:581
